TPU v7x, 128 devices: a whole 4x4x4 slice. The times are simulated.
128 devices in a mesh: row: 16 (over z, y_hi, core), col: 8 (over y_lo, x).
Axes of the slice: x: 4, y: 4 (y_hi: 2, y_lo: 2; y = y_hi * 2 + y_lo), z: 4, core: 2. Of those that a mesh axis runs over, the one named last changes fastest.
Arguments:
- layer_input: bfloat16 [2, 8192, 1024], P(None, 'row', 'col'), may hold values from -96 to 96
- out_grad: bfloat16 [2, 8192, 1024], P(None, 'row', 'col'), may hold values from -6 to 6
- token_route: int32 [2, 8192], P(None, 'row'), may hold values from 0 to 8191, as said below
- seq_lengths: int32 [2, 16, 4], P(None, 'row'), may hold values from 0 to 512, as said below
- positions: int32 [2, 8192], P(None, 'row'), may hold values from 0 to 3580, as said below
- attn_gain: bfloat16 [1024], replicated, may hold values from 0.099609375 to 1.8984375
- query_weight: bfloat16 [1024, 2048], P('row', 'col'), may hold values from -0.1875 to 0.1875
- key_weight: bfloat16 [1024, 1024], P('row', 'col'), may hold values from -0.1875 to 0.1875
- value_weight: bfloat16 [1024, 1024], P('row', 'col'), may hold values from -0.1875 to 0.1875
- query_gain: bfloat16 [128], replicated, may hold values from 0.099609375 to 1.8984375
- key_gain: bfloat16 [128], replicated, may hold values from 0.099609375 to 1.8984375
- out_weight: bfloat16 [2048, 1024], P('col', 'row'), may hold values from -0.5 to 0.5
- mlp_gain: bfloat16 [1024], replicated, may hold values from 0.099609375 to 1.8984375
- gate_weight: bfloat16 [1024, 3072], P('row', 'col'), may hold values from -0.1875 to 0.1875
- up_weight: bfloat16 [1024, 3072], P('row', 'col'), may hold values from -0.1875 to 0.1875
- down_weight: bfloat16 [3072, 1024], P('col', 'row'), may hold values from -0.109375 to 0.109375
Outputs:
- layer_output: bfloat16 [2, 8192, 1024], P(None, 'row', 'col')
- input_grad: bfloat16 [2, 8192, 1024], P(None, 'row', 'col')
- attn_gain_grad: float32 [1024], replicated
- query_grad: float32 [1024, 2048], P('row', 'col')
- key_grad: float32 [1024, 1024], P('row', 'col')
- value_grad: float32 [1024, 1024], P('row', 'col')
- query_gain_grad: float32 [128], replicated
- key_gain_grad: float32 [128], replicated
- out_proj_grad: float32 [2048, 1024], P('col', 'row')
- mlp_gain_grad: float32 [1024], replicated
- gate_grad: float32 [1024, 3072], P('row', 'col')
- up_grad: float32 [1024, 3072], P('row', 'col')
- down_grad: float32 [3072, 1024], P('col', 'row')
Inputs may be any that keep to these rules, and one draw needn't show every extreme that they name: Each row of token_route holds every number from 0 to 8191 once. Each aligned block of 512 entries holds the same number of entries of every group (g * 512 to (g + 1) * 512 - 1). `seq_lengths`: each row of 4 lengths sums to 512; nonzero lengths come first and zeros mark unused slots. Some row holds a single sequence of 512 tokens. Within each sequence of the group layout, positions rise by 1 to 3 from one token to the next.
All inputs are finite; a program needn't handle non-finite values.
Results may differ from a plain program's by a relative error of at most 0.018.
Values may be sent and summed in bfloat16 or wider, within the bound.
No kernel may reach another device: no remote copies, remote signals or barrier semaphores. Data moves between devices by JAX's collectives and lax.ppermute only.
A program may use at most 128 MiB of HBM per device.

v0:
```python
import math
import jax
import jax.numpy as jnp
from jax import lax
from jax.sharding import PartitionSpec as P

D = 1024
HEAD_SIZE = 128
EPSILON = 1e-06
ROPE_BASE = 1000000.0
NEGATIVE = -1e30
BOTH = ("row", "col")
ROWS = 16
BF = jnp.bfloat16
F32 = jnp.float32


def flat(row, col):
    return row * 8 + col


SAME_X = [[0, 1, 2, 3], [4, 5, 6, 7]]
CORES = [[2 * k, 2 * k + 1] for k in range(8)]
PLANE = [
    [flat(2 * k + core, 4 * y_lo + x) for k in range(8) for y_lo in range(2)]
    for x in range(4)
    for core in range(2)
]


def dot(a, b, dims):
    return lax.dot_general(a, b, (dims, ((), ())), preferred_element_type=F32)


def nn(a, b):
    return dot(a, b, ((1,), (0,)))


def nt(a, b):
    return dot(a, b, ((1,), (1,)))


def tn(a, b):
    return dot(a, b, ((0,), (0,)))


def exchange(blocks, axis, groups=None):
    return lax.all_to_all(blocks, axis, 0, 0, axis_index_groups=groups, tiled=True)


def rotate(t):
    half = t.shape[-1] // 2
    return jnp.concatenate([-t[..., half:], t[..., :half]], axis=-1)


def unrotate(t):
    half = t.shape[-1] // 2
    return jnp.concatenate([t[..., half:], -t[..., :half]], axis=-1)


def collect_weight(shard):
    n = shard.shape[1]
    plane = exchange(jnp.broadcast_to(shard[None], (16, 64, n)), BOTH, PLANE)
    pair = exchange(jnp.broadcast_to(plane[None], (2, 16, 64, n)), "row", CORES)
    pair = pair.reshape(2, 8, 2, 64, n)
    return jnp.transpose(pair, (1, 0, 3, 2, 4)).reshape(1024, 2, n)


def reduce_weight(grad):
    n = grad.shape[2]
    parts = jnp.transpose(grad.reshape(8, 2, 64, 2, n), (1, 0, 3, 2, 4)).astype(BF)
    parts = exchange(parts, "row", CORES)
    half = (parts[0].astype(F32) + parts[1].astype(F32)).astype(BF)
    got = exchange(half.reshape(16, 64, n), BOTH, PLANE)
    return jnp.sum(got.astype(F32), axis=0)


def send_tokens(rows):
    parts = jnp.transpose(rows.reshape(2, ROWS, 32, 128), (1, 0, 2, 3))
    parts = jnp.broadcast_to(parts[:, :, None], (ROWS, 2, 4, 32, 128)).reshape(128, 32, 128)
    got = exchange(parts, BOTH).reshape(ROWS, 8, 32, 128)
    return jnp.transpose(got, (0, 2, 1, 3)).reshape(512, 1024)


def return_tokens(part):
    parts = jnp.transpose(part.astype(BF).reshape(ROWS, 32, 8, 128), (0, 2, 1, 3))
    got = exchange(parts.reshape(128, 32, 128), BOTH).reshape(ROWS, 2, 4, 32, 128)
    total = jnp.sum(got.astype(F32), axis=2)
    return jnp.transpose(total, (1, 0, 2, 3)).reshape(2, 512, 128)


def scatter_sum(part):
    parts = jnp.transpose(part.astype(BF).reshape(512, 2, 4, 128), (2, 0, 1, 3))
    got = exchange(parts, "col", SAME_X)
    return jnp.sum(got.astype(F32), axis=0)


def collect_features(mine):
    got = exchange(jnp.broadcast_to(mine[None], (4, 512, 2, 128)), "col", SAME_X)
    return jnp.transpose(got, (1, 2, 0, 3)).reshape(512, 1024)


def body(
    layer_input,
    out_grad,
    token_route,
    seq_lengths,
    positions,
    attn_gain,
    query_weight,
    key_weight,
    value_weight,
    query_gain,
    key_gain,
    out_weight,
    mlp_gain,
    gate_weight,
    up_weight,
    down_weight,
):
    col = lax.axis_index("col")
    y_lo = col // 4
    x = col % 4
    places = jnp.arange(512, dtype=jnp.int32)
    rank = jnp.sum((token_route[:, None, :] < token_route[:, :, None]).astype(jnp.int32), axis=2)
    chosen = places[None, :, None] == rank[:, None, :]
    pick = chosen.astype(BF)
    slots_out = jnp.sum(jnp.where(chosen, (token_route % 512)[:, None, :], 0), axis=2)
    slots_all = exchange(jnp.transpose(slots_out.reshape(2, ROWS, 32), (1, 0, 2)), "row")
    slots = lax.dynamic_index_in_dim(slots_all, y_lo, 1, keepdims=False).reshape(512)

    def sort_rows(table):
        return jnp.stack([nn(pick[m], table[m]).astype(BF) for m in range(2)])

    def unsort_rows(table):
        return jnp.stack([tn(pick[m], table[m].astype(BF)).astype(BF) for m in range(2)])

    inputs = send_tokens(sort_rows(layer_input))
    grads = send_tokens(sort_rows(out_grad))
    qkv_full = collect_weight(jnp.concatenate([query_weight, key_weight, value_weight], axis=1))
    rest_full = collect_weight(
        jnp.concatenate([out_weight.T, gate_weight, up_weight, down_weight.T], axis=1)
    )
    wq, wk, wv = (qkv_full[:, :, :256], qkv_full[:, :, 256:384], qkv_full[:, :, 384:])
    wq, wk, wv = (wq.reshape(1024, 512), wk.reshape(1024, 256), wv.reshape(1024, 256))
    wo, wg, wu, wd = (
        rest_full[:, :, :256].reshape(1024, 512),
        rest_full[:, :, 256:640].reshape(1024, 768),
        rest_full[:, :, 640:1024].reshape(1024, 768),
        rest_full[:, :, 1024:].reshape(1024, 768),
    )
    gain_one = attn_gain.astype(F32)
    gain_two = mlp_gain.astype(F32)
    query_scale = query_gain.astype(F32)
    key_scale = key_gain.astype(F32)
    lengths = lax.dynamic_index_in_dim(seq_lengths, y_lo, 0, keepdims=False)[0]
    bound_one = lengths[0]
    bound_two = bound_one + lengths[1]
    bound_three = bound_two + lengths[2]
    segment = (
        (slots >= bound_one).astype(jnp.int32)
        + (slots >= bound_two).astype(jnp.int32)
        + (slots >= bound_three).astype(jnp.int32)
    )
    allowed = (segment[:, None] == segment[None, :]) & (slots[None, :] <= slots[:, None])
    my_positions = lax.dynamic_index_in_dim(positions, y_lo, 0, keepdims=False)
    position = jnp.sum(
        jnp.where(slots[:, None] == places[None, :], my_positions[None, :], 0), axis=1
    )
    freq_steps = jnp.arange(0, HEAD_SIZE, 2).astype(F32) / HEAD_SIZE
    frequency = 1.0 / ROPE_BASE**freq_steps
    angles = position.astype(F32)[:, None] * frequency[None, :]
    angles = jnp.concatenate([angles, angles], axis=-1)
    cosine, sine = (jnp.cos(angles)[:, None, :], jnp.sin(angles)[:, None, :])
    input_float = inputs.astype(F32)
    scale_one = lax.rsqrt(jnp.mean(input_float * input_float, axis=-1, keepdims=True) + EPSILON)
    hat_one = input_float * scale_one
    normed_one = (hat_one * gain_one).astype(BF)
    query_proj = nn(normed_one, wq).reshape(512, 4, HEAD_SIZE)
    key_proj = nn(normed_one, wk).reshape(512, 2, HEAD_SIZE)
    value_rows = nn(normed_one, wv).astype(BF).reshape(512, 2, HEAD_SIZE)
    query_inv = lax.rsqrt(jnp.mean(query_proj * query_proj, axis=-1, keepdims=True) + EPSILON)
    query_hat = query_proj * query_inv
    query_norm = query_hat * query_scale
    key_inv = lax.rsqrt(jnp.mean(key_proj * key_proj, axis=-1, keepdims=True) + EPSILON)
    key_hat = key_proj * key_inv
    key_norm = key_hat * key_scale
    query_rows = (query_norm * cosine + rotate(query_norm) * sine).astype(BF)
    key_rows = (key_norm * cosine + rotate(key_norm) * sine).astype(BF)
    grouped = query_rows.reshape(512, 2, 2, HEAD_SIZE)
    scores = jnp.einsum("qkrd,tkd->krqt", grouped, key_rows, preferred_element_type=F32)
    scores = jnp.where(allowed[None, None], scores * (1.0 / math.sqrt(HEAD_SIZE)), NEGATIVE)
    row_top = jnp.max(scores, axis=-1, keepdims=True)
    exp_scores = jnp.exp(scores - row_top)
    softmax = exp_scores / jnp.sum(exp_scores, axis=-1, keepdims=True)
    softmax_low = softmax.astype(BF)
    attended = jnp.einsum("krqt,tkd->qkrd", softmax_low, value_rows, preferred_element_type=F32)
    attended = attended.astype(BF).reshape(512, 512)
    summed = scatter_sum(nt(attended, wo))
    my_input = lax.dynamic_index_in_dim(inputs.reshape(512, 2, 4, 128), x, 2, keepdims=False)
    resid_mine = my_input.astype(F32) + summed
    resid = collect_features(resid_mine.astype(BF)).astype(F32)
    scale_two = lax.rsqrt(jnp.mean(resid * resid, axis=-1, keepdims=True) + EPSILON)
    hat_two = resid * scale_two
    normed_two = (hat_two * gain_two).astype(BF)
    gate = nn(normed_two, wg)
    up = nn(normed_two, wu)
    sigma = jax.nn.sigmoid(gate)
    activated = gate * sigma
    hidden = (activated * up).astype(BF)
    mine_mask = (jnp.arange(8, dtype=jnp.int32) % 4 == x).astype(F32)[None, :, None]

    def place(mine):
        wide = jnp.broadcast_to(mine[:, :, None, :], (512, 2, 4, 128)).reshape(512, 8, 128)
        return (wide * mine_mask).reshape(512, 1024)

    output_home = return_tokens(nt(hidden, wd) + place(resid_mine))
    delta_hidden = nn(grads, wd)
    delta_gate = (delta_hidden * up * sigma * (1.0 + gate * (1.0 - sigma))).astype(BF)
    delta_up = (delta_hidden * activated).astype(BF)
    delta_two = nt(delta_gate, wg) + nt(delta_up, wu)
    mlp_gain_sum = jnp.sum(delta_two * hat_two, axis=0)
    scaled = delta_two * gain_two
    inner = jnp.mean(scaled * hat_two, axis=-1, keepdims=True)
    my_grad = lax.dynamic_index_in_dim(grads.reshape(512, 2, 4, 128), x, 2, keepdims=False)
    resid_delta = my_grad.astype(F32) + scatter_sum(scale_two * (scaled - hat_two * inner))
    resid_low = collect_features(resid_delta.astype(BF))
    delta_attended = nn(resid_low, wo).astype(BF).reshape(512, 2, 2, HEAD_SIZE)
    rest_grad = jnp.concatenate(
        [
            tn(resid_low, attended).reshape(1024, 2, 256),
            tn(normed_two, delta_gate).reshape(1024, 2, 384),
            tn(normed_two, delta_up).reshape(1024, 2, 384),
            tn(grads, hidden).reshape(1024, 2, 384),
        ],
        axis=2,
    )
    rest_total = reduce_weight(rest_grad)
    delta_probs = jnp.einsum(
        "qkrd,tkd->krqt", delta_attended, value_rows, preferred_element_type=F32
    )
    delta_value = jnp.einsum(
        "krqt,qkrd->tkd", softmax_low, delta_attended, preferred_element_type=F32
    )
    delta_scores = (
        softmax * (delta_probs - jnp.sum(delta_probs * softmax, axis=-1, keepdims=True))
    ).astype(BF)
    delta_query = jnp.einsum(
        "krqt,tkd->qkrd", delta_scores, key_rows, preferred_element_type=F32
    ) * (1.0 / math.sqrt(HEAD_SIZE))
    delta_key = jnp.einsum("krqt,qkrd->tkd", delta_scores, grouped, preferred_element_type=F32) * (
        1.0 / math.sqrt(HEAD_SIZE)
    )
    delta_query = delta_query.reshape(512, 4, HEAD_SIZE)
    delta_query_norm = delta_query * cosine + unrotate(delta_query * sine)
    delta_key_norm = delta_key * cosine + unrotate(delta_key * sine)
    query_gain_sum = jnp.sum(delta_query_norm * query_hat, axis=(0, 1))
    key_gain_sum = jnp.sum(delta_key_norm * key_hat, axis=(0, 1))

    def norm_back(delta, hat, inv, gain):
        part = delta * gain
        part = inv * (part - hat * jnp.mean(part * hat, axis=-1, keepdims=True))
        return part.astype(BF).reshape(512, -1)

    delta_query_proj = norm_back(delta_query_norm, query_hat, query_inv, query_scale)
    delta_key_proj = norm_back(delta_key_norm, key_hat, key_inv, key_scale)
    delta_value_proj = delta_value.astype(BF).reshape(512, -1)
    delta_one = nt(delta_query_proj, wq) + nt(delta_key_proj, wk) + nt(delta_value_proj, wv)
    attn_gain_sum = jnp.sum(delta_one * hat_one, axis=0)
    scaled = delta_one * gain_one
    inner = jnp.mean(scaled * hat_one, axis=-1, keepdims=True)
    delta_home = return_tokens(scale_one * (scaled - hat_one * inner) + place(resid_delta))
    qkv_grad = jnp.concatenate(
        [
            tn(normed_one, delta_query_proj).reshape(1024, 2, 256),
            tn(normed_one, delta_key_proj).reshape(1024, 2, 128),
            tn(normed_one, delta_value_proj).reshape(1024, 2, 128),
        ],
        axis=2,
    )
    qkv_total = reduce_weight(qkv_grad)
    attn_gain_grad, mlp_gain_grad, query_gain_grad, key_gain_grad = lax.psum(
        (attn_gain_sum, mlp_gain_sum, query_gain_sum, key_gain_sum), BOTH
    )
    return (
        unsort_rows(output_home),
        unsort_rows(delta_home),
        attn_gain_grad,
        qkv_total[:, :256],
        qkv_total[:, 256:384],
        qkv_total[:, 384:],
        query_gain_grad,
        key_gain_grad,
        rest_total[:, :256].T,
        mlp_gain_grad,
        rest_total[:, 256:640],
        rest_total[:, 640:1024],
        rest_total[:, 1024:].T,
    )


def solution(mesh):
    in_specs = (
        P(None, "row", "col"),
        P(None, "row", "col"),
        P(None, "row"),
        P(None, "row", None),
        P(None, "row"),
        P(),
        P("row", "col"),
        P("row", "col"),
        P("row", "col"),
        P(),
        P(),
        P("col", "row"),
        P(),
        P("row", "col"),
        P("row", "col"),
        P("col", "row"),
    )
    out_specs = (
        P(None, "row", "col"),
        P(None, "row", "col"),
        P(),
        P("row", "col"),
        P("row", "col"),
        P("row", "col"),
        P(),
        P(),
        P("col", "row"),
        P(),
        P("row", "col"),
        P("row", "col"),
        P("col", "row"),
    )
    return jax.shard_map(body, mesh=mesh, in_specs=in_specs, out_specs=out_specs, check_vma=False)
```

profile of v0, /device:TPU:1, one launch (start us, length us, event | category | flops | bytes accessed | tf_op | source)
XLA Modules:
  0.0 547.3 jit_solution(2396641583294308032)
XLA Ops:
  3.5 9.5 %all-to-all-start.3 = ((s32[16,2,32]{2,1,0:T(2,128)}), s32[16,2,32]{2,1,0:T(2,128)S(1)}, u32[]{:S(2)}, u32[]{:S(2)}) async-start(s32[16,2,32]{2,1,0:T(2,128)} %copy.266), calls=%async_computation.3 | async-start | bytes 32768 | tf_op jit(solution)/shard_map/all_to_all | solution.py:48
  17.0 3.3 all-to-all-done.3
  21.4 3.7 all-to-all-start.1
  29.6 12.3 %all-to-all-done.1 = bf16[16,64,512]{2,1,0:T(8,128)(2,1)S(1)} async-done(((bf16[16,64,512]{2,1,0:T(8,128)(2,1)}), bf16[16,64,512]{2,1,0:T(8,128)(2,1)S(1)}, u32[]{:S(2)}, u32[]{:S(2)}) %all-to-all-start.1) | async-done | bytes 1048608 | tf_op jit(solution)/shard_map/all_to_all | solution.py:48
  42.1 6.9 %all_to_all.85 = bf16[2,16,64,512]{3,2,1,0:T(8,128)(2,1)S(1)} all-to-all(bf16[2,16,64,512]{3,2,1,0:T(8,128)(2,1)S(1)} %broadcast_in_dim.60), channel_id=1, replica_groups={{0,8},{16,24},{32,40},{48,56},{64,72},{80,88},{96,104},{112,120},{1,9},..., dimensions={0} | all-to-all | bytes 4194304 | tf_op jit(solution)/shard_map/all_to_all | solution.py:48
  50.2 5.5 all-to-all-start
  64.1 11.0 %all-to-all-done = bf16[128,32,128]{2,1,0:T(8,128)(2,1)S(1)} async-done(((bf16[128,32,128]{2,1,0:T(8,128)(2,1)}), bf16[128,32,128]{2,1,0:T(8,128)(2,1)S(1)}, u32[]{:S(2)}, u32[]{:S(2)}) %all-to-all-start) | async-done | bytes 1048608 | tf_op jit(solution)/shard_map/all_to_all | solution.py:48
  77.0 4.7 all-to-all-start.4
  89.2 3.7 fusion.83
  92.9 31.9 %all-to-all-done.4 = bf16[16,64,1408]{2,1,0:T(8,128)(2,1)} async-done(((bf16[16,64,1408]{2,1,0:T(8,128)(2,1)}), bf16[16,64,1408]{2,1,0:T(8,128)(2,1)}, u32[]{:S(2)}, u32[]{:S(2)}) %all-to-all-start.4) | async-done | bytes 2883616 | tf_op jit(solution)/shard_map/all_to_all | solution.py:48
  127.4 10.9 %all_to_all.86 = bf16[2,16,64,1408]{3,2,1,0:T(8,128)(2,1)} all-to-all(bf16[2,16,64,1408]{3,2,1,0:T(8,128)(2,1)S(1)} %broadcast_in_dim.73), channel_id=1, replica_groups={{0,8},{16,24},{32,40},{48,56},{64,72},{80,88},{96,104},{112,120},{1,9},..., dimensions={0} | all-to-all | bytes 11534336 | tf_op jit(solution)/shard_map/all_to_all | solution.py:48
  139.4 5.6 %all-to-all-start.9 = ((bf16[128,32,128]{2,1,0:T(8,128)(2,1)}), bf16[128,32,128]{2,1,0:T(8,128)(2,1)S(1)}, u32[]{:S(2)}, u32[]{:S(2)}) async-start(bf16[128,32,128]{2,1,0:T(8,128)(2,1)} %bitcast.399), calls=%async_computation.9 | async-start | bytes 2097152 | tf_op jit(solution)/shard_map/all_to_all | solution.py:48
  147.1 3.6 convolution_convert_fusion.8
  157.1 3.1 convolution_convert_fusion.5
  162.8 3.0 copy.386
  165.8 4.3 all-to-all-start.6
  189.4 4.7 all-to-all-start.7
  194.2 4.6 fusion.73
  206.6 4.0 fusion.26
  212.8 3.1 reshape.607
  215.9 3.7 copy.277
  231.3 3.1 fusion.14
  242.0 3.0 copy.385
  245.0 4.4 all-to-all-start.10
  249.4 4.1 fusion.19
  262.0 3.7 convolution_convert_fusion.1
  270.8 4.3 all-to-all-start.11
  275.1 3.7 convolution_convert_fusion.2
  283.3 3.1 reshape.618
  286.9 3.6 copy.290
  295.4 3.9 fusion.20
  304.8 4.6 fusion.3
  318.3 3.9 copy.300
  322.2 3.2 copy.301
  325.4 9.3 %all-to-all-start.13 = ((bf16[2,8,2,64,512]{4,3,1,2,0:T(8,128)(2,1)}), bf16[2,8,2,64,512]{4,3,1,2,0:T(8,128)(2,1)}, u32[]{:S(2)}, u32[]{:S(2)}) async-start(bf16[2,8,2,64,512]{4,3,1,2,0:T(8,128)(2,1)} %copy.301), calls=%async_computation.13 | async-start | bytes 4194304 | tf_op jit(solution)/shard_map/all_to_all | solution.py:48
  336.6 5.1 pad_maximum_fusion
  341.6 8.4 %all-to-all-start.8 = ((bf16[128,32,128]{2,1,0:T(8,128)(2,1)}), bf16[128,32,128]{2,1,0:T(8,128)(2,1)S(1)}, u32[]{:S(2)}, u32[]{:S(2)}) async-start(bf16[128,32,128]{2,1,0:T(8,128)(2,1)} %bitcast.400), calls=%async_computation.8 | async-start | bytes 2097152 | tf_op jit(solution)/shard_map/all_to_all | solution.py:48
  353.0 8.3 %copy.309 = bf16[1024,2,1408]{2,0,1:T(8,128)(2,1)} copy(bf16[1024,2,1408]{0,2,1:T(8,128)(2,1)} %pad_maximum_fusion) | data formatting | bytes 11534336 | tf_op jit(solution)/shard_map/concatenate | solution.py:229
  361.3 5.7 %copy.310 = bf16[2,8,2,64,1408]{4,3,1,2,0:T(8,128)(2,1)} copy(bf16[2,8,2,64,1408]{4,3,0,1,2:T(8,128)(2,1)} %bitcast.384) | data formatting | bytes 11534336 | tf_op jit(solution)/shard_map/convert_element_type | solution.py:71
  372.4 15.2 %all_to_all.87 = bf16[2,8,2,64,1408]{4,3,1,2,0:T(8,128)(2,1)} all-to-all(bf16[2,8,2,64,1408]{4,3,1,2,0:T(8,128)(2,1)} %copy.310), channel_id=1, replica_groups={{0,8},{16,24},{32,40},{48,56},{64,72},{80,88},{96,104},{112,120},{1,9},..., dimensions={0} | all-to-all | bytes 11534336 | tf_op jit(solution)/shard_map/all_to_all | solution.py:48
  387.6 6.9 %all-to-all-start.14 = ((bf16[16,64,512]{2,1,0:T(8,128)(2,1)}), bf16[16,64,512]{2,1,0:T(8,128)(2,1)S(1)}, u32[]{:S(2)}, u32[]{:S(2)}) async-start(bf16[16,64,512]{2,1,0:T(8,128)(2,1)} %bitcast.114), calls=%async_computation.14 | async-start | bytes 2097152 | tf_op jit(solution)/shard_map/all_to_all | solution.py:48
  394.5 3.9 multiply_reduce_fusion.1
  400.8 10.0 %all-to-all-done.14 = bf16[16,64,512]{2,1,0:T(8,128)(2,1)S(1)} async-done(((bf16[16,64,512]{2,1,0:T(8,128)(2,1)}), bf16[16,64,512]{2,1,0:T(8,128)(2,1)S(1)}, u32[]{:S(2)}, u32[]{:S(2)}) %all-to-all-start.14) | async-done | bytes 1048608 | tf_op jit(solution)/shard_map/all_to_all | solution.py:48
  410.8 7.2 %all-to-all-start.12 = ((bf16[128,32,128]{2,1,0:T(8,128)(2,1)}), bf16[128,32,128]{2,1,0:T(8,128)(2,1)S(1)}, u32[]{:S(2)}, u32[]{:S(2)}) async-start(bf16[128,32,128]{2,1,0:T(8,128)(2,1)} %bitcast.97), calls=%async_computation.12 | async-start | bytes 2097152 | tf_op jit(solution)/shard_map/all_to_all | solution.py:48
  418.0 3.1 fusion.72
  423.6 13.8 %all-to-all-done.12 = bf16[128,32,128]{2,1,0:T(8,128)(2,1)S(1)} async-done(((bf16[128,32,128]{2,1,0:T(8,128)(2,1)}), bf16[128,32,128]{2,1,0:T(8,128)(2,1)S(1)}, u32[]{:S(2)}, u32[]{:S(2)}) %all-to-all-start.12) | async-done | bytes 1048608 | tf_op jit(solution)/shard_map/all_to_all | solution.py:48
  438.5 3.7 all-to-all-start.16
  445.4 94.9 %all-reduce = (f32[1024]{0:T(1024)}, f32[128]{0:T(128)}, f32[128]{0:T(128)}, f32[1024]{0:T(1024)}) all-reduce(f32[1024]{0:T(1024)S(1)} %get-tuple-element.15, f32[128]{0:T(128)S(1)} %get-tuple-element.17, f32[128]{0:T(128)S(1)} %get-tuple-element.19, f32[1024]{0:T(1024)S(1)} %get-tuple-element.13), channel_id=1, replica_groups=mesh['row'=16,'col'=8] {'row','col'}, use_global_device_ids=true, to_apply=%region_19.20 | all-reduce | flops 2304 | bytes 18432 | tf_op jit(solution)/shard_map/psum | solution.py:282
  (296 shorter events, 155.8 us)
Async XLA Ops:
  0.6 27.8 %copy-start = (s32[2,512]{1,0:T(2,128)S(1)}, s32[2,512]{1,0:T(2,128)}, u32[]{:S(2)}) copy-start(s32[2,512]{1,0:T(2,128)} %param.20) | copy-start | bytes 12292
  0.7 15.4 %copy-start.58 = (bf16[2,512,128]{2,1,0:T(8,128)(2,1)S(1)}, bf16[2,512,128]{2,1,0:T(8,128)(2,1)}, u32[]{:S(2)}) copy-start(bf16[2,512,128]{2,1,0:T(8,128)(2,1)} %param.17) | copy-start | bytes 786436
  3.5 16.8 %all-to-all-start.3 = ((s32[16,2,32]{2,1,0:T(2,128)}), s32[16,2,32]{2,1,0:T(2,128)S(1)}, u32[]{:S(2)}, u32[]{:S(2)}) async-start(s32[16,2,32]{2,1,0:T(2,128)} %copy.266), calls=%async_computation.3 | async-start | bytes 32768 | tf_op jit(solution)/shard_map/all_to_all | solution.py:48
  13.3 3.4 copy-start.45
  16.7 8.3 %copy-start.59 = (s32[2,1,4]{2,1,0:T(1,128)S(1)}, s32[2,1,4]{2,1,0:T(1,128)}, u32[]{:S(2)}) copy-start(s32[2,1,4]{2,1,0:T(1,128)} %param.19) | copy-start | bytes 100
  16.8 8.3 %copy-start.60 = (bf16[128]{0:T(256)(128)(2,1)S(1)}, bf16[128]{0:T(256)(128)(2,1)}, u32[]{:S(2)}) copy-start(bf16[128]{0:T(256)(128)(2,1)} %param.26) | copy-start | bytes 772
  16.8 8.3 %copy-start.61 = (bf16[128]{0:T(256)(128)(2,1)S(1)}, bf16[128]{0:T(256)(128)(2,1)}, u32[]{:S(2)}) copy-start(bf16[128]{0:T(256)(128)(2,1)} %param.25) | copy-start | bytes 772
  16.9 11.6 %copy-start.56 = (bf16[1024]{0:T(1024)(128)(2,1)S(1)}, bf16[1024]{0:T(1024)(128)(2,1)}, u32[]{:S(2)}) copy-start(bf16[1024]{0:T(1024)(128)(2,1)} %param.21) | copy-start | bytes 6148
  16.9 11.6 %copy-start.49 = (bf16[384,64]{0,1:T(8,128)(2,1)S(1)}, bf16[384,64]{0,1:T(8,128)(2,1)}, u32[]{:S(2)}) copy-start(bf16[384,64]{0,1:T(8,128)(2,1)} %param.31) | copy-start | bytes 147460
  16.9 11.6 %copy-start.50 = (bf16[64,384]{1,0:T(8,128)(2,1)S(1)}, bf16[64,384]{1,0:T(8,128)(2,1)}, u32[]{:S(2)}) copy-start(bf16[64,384]{1,0:T(8,128)(2,1)} %param.30) | copy-start | bytes 147460
  16.9 11.6 %copy-start.51 = (bf16[64,384]{1,0:T(8,128)(2,1)S(1)}, bf16[64,384]{1,0:T(8,128)(2,1)}, u32[]{:S(2)}) copy-start(bf16[64,384]{1,0:T(8,128)(2,1)} %param.29) | copy-start | bytes 147460
  17.0 11.6 %copy-start.53 = (bf16[256,64]{0,1:T(8,128)(2,1)S(1)}, bf16[256,64]{0,1:T(8,128)(2,1)}, u32[]{:S(2)}) copy-start(bf16[256,64]{0,1:T(8,128)(2,1)} %param.27) | copy-start | bytes 98308
  21.4 20.5 %all-to-all-start.1 = ((bf16[16,64,512]{2,1,0:T(8,128)(2,1)}), bf16[16,64,512]{2,1,0:T(8,128)(2,1)S(1)}, u32[]{:S(2)}, u32[]{:S(2)}) async-start(bf16[16,64,512]{2,1,0:T(8,128)(2,1)} %broadcast_in_dim.59), calls=%async_computation.1 | async-start | bytes 2097152 | tf_op jit(solution)/shard_map/all_to_all | solution.py:48
  50.2 24.9 %all-to-all-start = ((bf16[128,32,128]{2,1,0:T(8,128)(2,1)}), bf16[128,32,128]{2,1,0:T(8,128)(2,1)S(1)}, u32[]{:S(2)}, u32[]{:S(2)}) async-start(bf16[128,32,128]{2,1,0:T(8,128)(2,1)} %bitcast.398), calls=%async_computation | async-start | bytes 2097152 | tf_op jit(solution)/shard_map/all_to_all | solution.py:48
  61.7 13.3 %copy-start.44 = (bf16[64,1408]{1,0:T(8,128)(2,1)S(1)}, bf16[64,1408]{1,0:T(8,128)(2,1)}, u32[]{:S(2)}) copy-start(bf16[64,1408]{1,0:T(8,128)(2,1)} %pad_maximum_fusion.5) | copy-start | bytes 540676
  77.0 47.9 %all-to-all-start.4 = ((bf16[16,64,1408]{2,1,0:T(8,128)(2,1)}), bf16[16,64,1408]{2,1,0:T(8,128)(2,1)}, u32[]{:S(2)}, u32[]{:S(2)}) async-start(bf16[16,64,1408]{2,1,0:T(8,128)(2,1)} %broadcast_in_dim.72), calls=%async_computation.4 | async-start | bytes 5767168 | tf_op jit(solution)/shard_map/all_to_all | solution.py:48
  83.3 2.8 copy-start.4
  88.6 4.3 copy-start.29
  127.4 10.9 %copy-start.37 = (bf16[16,2,32,128]{3,2,1,0:T(8,128)(2,1)S(1)}, bf16[16,2,32,128]{3,2,1,0:T(8,128)(2,1)}, u32[]{:S(2)}) copy-start(bf16[16,2,32,128]{3,2,1,0:T(8,128)(2,1)} %copy.282) | copy-start | bytes 786436
  139.4 26.4 %all-to-all-start.9 = ((bf16[128,32,128]{2,1,0:T(8,128)(2,1)}), bf16[128,32,128]{2,1,0:T(8,128)(2,1)S(1)}, u32[]{:S(2)}, u32[]{:S(2)}) async-start(bf16[128,32,128]{2,1,0:T(8,128)(2,1)} %bitcast.399), calls=%async_computation.9 | async-start | bytes 2097152 | tf_op jit(solution)/shard_map/all_to_all | solution.py:48
  145.1 5.6 %slice-start = ((s8[5767168]{0:T(1024)(128)(4,1)}), s8[4194304]{0:T(1024)(128)(4,1)S(1)}, s32[]{:S(2)}) async-start(s8[5767168]{0:T(1024)(128)(4,1)} %bitcast.381), calls=%async_computation.17 | async-start | bytes 8388608
  147.1 3.6 copy-start.62
  147.1 3.6 slice-start.1
  162.8 7.3 %copy-start.57 = (bf16[1024]{0:T(1024)(128)(2,1)S(1)}, bf16[1024]{0:T(1024)(128)(2,1)}, u32[]{:S(2)}) copy-start(bf16[1024]{0:T(1024)(128)(2,1)} %param.28) | copy-start | bytes 6148
  165.8 18.4 %all-to-all-start.6 = ((bf16[4,512,2,128]{3,2,1,0:T(2,128)(2,1)}), bf16[4,512,2,128]{3,2,1,0:T(2,128)(2,1)}, u32[]{:S(2)}, u32[]{:S(2)}) async-start(bf16[4,512,2,128]{3,2,1,0:T(2,128)(2,1)} %bitcast.403), calls=%async_computation.6 | async-start | bytes 2097152 | tf_op jit(solution)/shard_map/all_to_all | solution.py:48
  189.4 26.5 %all-to-all-start.7 = ((bf16[4,512,2,128]{3,2,1,0:T(2,128)(2,1)}), bf16[4,512,2,128]{3,2,1,0:T(2,128)(2,1)}, u32[]{:S(2)}, u32[]{:S(2)}) async-start(bf16[4,512,2,128]{3,2,1,0:T(2,128)(2,1)} %broadcast_in_dim.74), calls=%async_computation.7 | async-start | bytes 2097152 | tf_op jit(solution)/shard_map/all_to_all | solution.py:48
  206.6 4.0 copy-start.11
  206.6 4.0 copy-start.25
  229.6 4.8 copy-start.65
  245.0 20.6 %all-to-all-start.10 = ((bf16[4,512,2,128]{3,2,1,0:T(2,128)(2,1)}), bf16[4,512,2,128]{3,2,1,0:T(2,128)(2,1)}, u32[]{:S(2)}, u32[]{:S(2)}) async-start(bf16[4,512,2,128]{3,2,1,0:T(2,128)(2,1)} %bitcast.404), calls=%async_computation.10 | async-start | bytes 2097152 | tf_op jit(solution)/shard_map/all_to_all | solution.py:48
  270.8 16.1 %all-to-all-start.11 = ((bf16[4,512,2,128]{3,2,1,0:T(2,128)(2,1)}), bf16[4,512,2,128]{3,2,1,0:T(2,128)(2,1)}, u32[]{:S(2)}, u32[]{:S(2)}) async-start(bf16[4,512,2,128]{3,2,1,0:T(2,128)(2,1)} %broadcast_in_dim.78), calls=%async_computation.11 | async-start | bytes 2097152 | tf_op jit(solution)/shard_map/all_to_all | solution.py:48
  275.1 3.8 copy-start.38
  275.1 3.7 copy-start.43
  295.4 3.9 copy-start.14
  295.4 3.9 copy-start.63
  304.8 4.6 copy-start.42
  325.4 9.3 %copy-start.39 = (bf16[512,1024,1]{1,0,2:T(8,128)(2,1)S(1)}, bf16[512,1024,1]{1,0,2:T(8,128)(2,1)}, u32[]{:S(2)}) copy-start(bf16[512,1024,1]{1,0,2:T(8,128)(2,1)} %reshape.638) | copy-start | bytes 3145732
  325.4 16.2 %all-to-all-start.13 = ((bf16[2,8,2,64,512]{4,3,1,2,0:T(8,128)(2,1)}), bf16[2,8,2,64,512]{4,3,1,2,0:T(8,128)(2,1)}, u32[]{:S(2)}, u32[]{:S(2)}) async-start(bf16[2,8,2,64,512]{4,3,1,2,0:T(8,128)(2,1)} %copy.301), calls=%async_computation.13 | async-start | bytes 4194304 | tf_op jit(solution)/shard_map/all_to_all | solution.py:48
  341.6 30.7 %all-to-all-start.8 = ((bf16[128,32,128]{2,1,0:T(8,128)(2,1)}), bf16[128,32,128]{2,1,0:T(8,128)(2,1)S(1)}, u32[]{:S(2)}, u32[]{:S(2)}) async-start(bf16[128,32,128]{2,1,0:T(8,128)(2,1)} %bitcast.400), calls=%async_computation.8 | async-start | bytes 2097152 | tf_op jit(solution)/shard_map/all_to_all | solution.py:48
  372.4 15.2 %copy-start.17 = (bf16[128,32,128]{2,1,0:T(8,128)(2,1)}, bf16[128,32,128]{2,1,0:T(8,128)(2,1)S(1)}, u32[]{:S(2)}) copy-start(bf16[128,32,128]{2,1,0:T(8,128)(2,1)S(1)} %all-to-all-done.8) | copy-start | bytes 3145732
  387.6 6.9 %copy-start.35 = (bf16[2,128,512]{2,1,0:T(8,128)(2,1)S(1)}, bf16[2,128,512]{2,1,0:T(8,128)(2,1)}, u32[]{:S(2)}) copy-start(bf16[2,128,512]{2,1,0:T(8,128)(2,1)} %fusion.20) | copy-start | bytes 786436
  387.6 23.2 %all-to-all-start.14 = ((bf16[16,64,512]{2,1,0:T(8,128)(2,1)}), bf16[16,64,512]{2,1,0:T(8,128)(2,1)S(1)}, u32[]{:S(2)}, u32[]{:S(2)}) async-start(bf16[16,64,512]{2,1,0:T(8,128)(2,1)} %bitcast.114), calls=%async_computation.14 | async-start | bytes 2097152 | tf_op jit(solution)/shard_map/all_to_all | solution.py:48
  394.5 3.9 copy-start.7
  410.8 10.3 %copy-start.20 = (bf16[16,64,512]{2,1,0:T(8,128)(2,1)}, bf16[16,64,512]{2,1,0:T(8,128)(2,1)S(1)}, u32[]{:S(2)}) copy-start(bf16[16,64,512]{2,1,0:T(8,128)(2,1)S(1)} %all-to-all-done.14) | copy-start | bytes 3145732
  410.8 26.6 %all-to-all-start.12 = ((bf16[128,32,128]{2,1,0:T(8,128)(2,1)}), bf16[128,32,128]{2,1,0:T(8,128)(2,1)S(1)}, u32[]{:S(2)}, u32[]{:S(2)}) async-start(bf16[128,32,128]{2,1,0:T(8,128)(2,1)} %bitcast.97), calls=%async_computation.12 | async-start | bytes 2097152 | tf_op jit(solution)/shard_map/all_to_all | solution.py:48
  437.5 6.2 %copy-start.46 = (pred[2,512,512]{2,1,0:T(32,128)(4,1)S(1)}, pred[2,512,512]{2,1,0:T(32,128)(4,1)}, u32[]{:S(2)}) copy-start(pred[2,512,512]{2,1,0:T(32,128)(4,1)} %copy-done.45) | copy-start | bytes 1572868
  438.5 106.6 %all-to-all-start.16 = ((bf16[16,64,1408]{2,1,0:T(8,128)(2,1)}), bf16[16,64,1408]{2,1,0:T(8,128)(2,1)S(1)}, u32[]{:S(2)}, u32[]{:S(2)}) async-start(bf16[16,64,1408]{2,1,0:T(8,128)(2,1)} %bitcast.128), calls=%async_computation.16 | async-start | bytes 5767168 | tf_op jit(solution)/shard_map/all_to_all | solution.py:48
  540.2 2.8 copy-start.19
  (35 other events, 55.0 us)
where the time goes:
time: 556 us; the launch traced here: 547 us
  local copies, waits for them, and re-layouts  134 us (24%)
  blocking collectives  128 us (23%)
  waiting for transfers between devices  85.7 us (15%)
  starting transfers between devices  82.1 us (15%)
  matrix products  68.2 us (12%)
  other arithmetic  45.3 us (8%)
    psum x1, blocking collectives, body(): lax.psum((attn_gain_sum, mlp_gain_sum, query_gain_sum, key_gain_sum), BOTH)  94.9 us
    all_to_all x14, waiting for transfers between devices, exchange(): lax.all_to_all(blocks, axis, 0, 0, axis_index_groups=groups, tiled=True)  85.7 us
    all_to_all x14, starting transfers between devices, exchange(): lax.all_to_all(blocks, axis, 0, 0, axis_index_groups=groups, tiled=True)  82.1 us
    dot_general x29, matrix products, dot(): return lax.dot_general(a, b, (dims, ((), ())), preferred_element_type=F32)  53 us
    all_to_all x3, blocking collectives, exchange(): lax.all_to_all(blocks, axis, 0, 0, axis_index_groups=groups, tiled=True)  33 us
    unnamed x140, local copies, waits for them, and re-layouts  13.9 us
    reshape x4, local copies, waits for them, and re-layouts, scatter_sum(): parts = jnp.transpose(part.astype(BF).reshape(512, 2, 4, 128), (2, 0, 1, 3))  11.2 us
  transfers between devices with their start and end apart: 14, of which 8 were waited for; matrix products, arithmetic and copies ran while one was open for 27% of the time, Pallas kernels for 0%

commit v1 on v0

--- a/solution.py
+++ b/solution.py
@@ -280,7 +280,7 @@
     )
     qkv_total = reduce_weight(qkv_grad)
     attn_gain_grad, mlp_gain_grad, query_gain_grad, key_gain_grad = lax.psum(
-        (attn_gain_sum, mlp_gain_sum, query_gain_sum, key_gain_sum), BOTH
+        lax.psum((attn_gain_sum, mlp_gain_sum, query_gain_sum, key_gain_sum), "row"), "col"
     )
     return (
         unsort_rows(output_home),

time: 556 us -> 550 us (0.989)
  the two profiles are of different devices: /device:TPU:1 before, /device:TPU:0 now
where the time goes in v1:
time: 550 us; the launch traced here: 541 us
  local copies, waits for them, and re-layouts  132 us (24%)
  blocking collectives  119 us (22%)
  waiting for transfers between devices  91.4 us (17%)
  starting transfers between devices  79.2 us (14%)
  matrix products  68.1 us (12%)
  other arithmetic  46.3 us (8%)
    all_to_all x14, waiting for transfers between devices, exchange(): lax.all_to_all(blocks, axis, 0, 0, axis_index_groups=groups, tiled=True)  91.4 us
    all_to_all x14, starting transfers between devices, exchange(): lax.all_to_all(blocks, axis, 0, 0, axis_index_groups=groups, tiled=True)  79.2 us
    psum x1, blocking collectives, body(): lax.psum((attn_gain_sum, mlp_gain_sum, query_gain_sum, key_gain_sum), 'row')  66.8 us
    dot_general x29, matrix products, dot(): return lax.dot_general(a, b, (dims, ((), ())), preferred_element_type=F32)  53 us
    all_to_all x3, blocking collectives, exchange(): lax.all_to_all(blocks, axis, 0, 0, axis_index_groups=groups, tiled=True)  29.6 us
    psum x1, blocking collectives, body(): lax.psum(lax.psum((attn_gain_sum, mlp_gain_sum, query_gain_sum, key_gain_...  22.7 us
    unnamed x140, local copies, waits for them, and re-layouts  12.8 us
    reshape x4, local copies, waits for them, and re-layouts, scatter_sum(): parts = jnp.transpose(part.astype(BF).reshape(512, 2, 4, 128), (2, 0, 1, 3))  11.2 us
  transfers between devices with their start and end apart: 14, of which 8 were waited for; matrix products, arithmetic and copies ran while one was open for 28% of the time, Pallas kernels for 0%

profile of v1, /device:TPU:0, one launch (start us, length us, event | category | flops | bytes accessed | tf_op | source)
XLA Modules:
  0.0 540.9 jit_solution(10745203296987070405)
XLA Ops:
  3.5 8.1 %all-to-all-start.3 = ((s32[16,2,32]{2,1,0:T(2,128)}), s32[16,2,32]{2,1,0:T(2,128)S(1)}, u32[]{:S(2)}, u32[]{:S(2)}) async-start(s32[16,2,32]{2,1,0:T(2,128)} %copy.266), calls=%async_computation.3 | async-start | bytes 32768 | tf_op jit(solution)/shard_map/all_to_all | solution.py:48
  15.6 3.6 all-to-all-done.3
  20.4 3.7 all-to-all-start.1
  28.5 13.8 %all-to-all-done.1 = bf16[16,64,512]{2,1,0:T(8,128)(2,1)S(1)} async-done(((bf16[16,64,512]{2,1,0:T(8,128)(2,1)}), bf16[16,64,512]{2,1,0:T(8,128)(2,1)S(1)}, u32[]{:S(2)}, u32[]{:S(2)}) %all-to-all-start.1) | async-done | bytes 1048608 | tf_op jit(solution)/shard_map/all_to_all | solution.py:48
  42.6 5.4 %all_to_all.85 = bf16[2,16,64,512]{3,2,1,0:T(8,128)(2,1)S(1)} all-to-all(bf16[2,16,64,512]{3,2,1,0:T(8,128)(2,1)S(1)} %broadcast_in_dim.60), channel_id=1, replica_groups={{0,8},{16,24},{32,40},{48,56},{64,72},{80,88},{96,104},{112,120},{1,9},..., dimensions={0} | all-to-all | bytes 4194304 | tf_op jit(solution)/shard_map/all_to_all | solution.py:48
  49.1 6.2 %all-to-all-start = ((bf16[128,32,128]{2,1,0:T(8,128)(2,1)}), bf16[128,32,128]{2,1,0:T(8,128)(2,1)S(1)}, u32[]{:S(2)}, u32[]{:S(2)}) async-start(bf16[128,32,128]{2,1,0:T(8,128)(2,1)} %bitcast.398), calls=%async_computation | async-start | bytes 2097152 | tf_op jit(solution)/shard_map/all_to_all | solution.py:48
  63.7 10.8 %all-to-all-done = bf16[128,32,128]{2,1,0:T(8,128)(2,1)S(1)} async-done(((bf16[128,32,128]{2,1,0:T(8,128)(2,1)}), bf16[128,32,128]{2,1,0:T(8,128)(2,1)S(1)}, u32[]{:S(2)}, u32[]{:S(2)}) %all-to-all-start) | async-done | bytes 1048608 | tf_op jit(solution)/shard_map/all_to_all | solution.py:48
  76.3 4.7 all-to-all-start.4
  88.6 3.7 fusion.83
  92.3 32.7 %all-to-all-done.4 = bf16[16,64,1408]{2,1,0:T(8,128)(2,1)} async-done(((bf16[16,64,1408]{2,1,0:T(8,128)(2,1)}), bf16[16,64,1408]{2,1,0:T(8,128)(2,1)}, u32[]{:S(2)}, u32[]{:S(2)}) %all-to-all-start.4) | async-done | bytes 2883616 | tf_op jit(solution)/shard_map/all_to_all | solution.py:48
  127.6 9.6 %all_to_all.86 = bf16[2,16,64,1408]{3,2,1,0:T(8,128)(2,1)} all-to-all(bf16[2,16,64,1408]{3,2,1,0:T(8,128)(2,1)S(1)} %broadcast_in_dim.73), channel_id=1, replica_groups={{0,8},{16,24},{32,40},{48,56},{64,72},{80,88},{96,104},{112,120},{1,9},..., dimensions={0} | all-to-all | bytes 11534336 | tf_op jit(solution)/shard_map/all_to_all | solution.py:48
  138.4 6.3 %all-to-all-start.9 = ((bf16[128,32,128]{2,1,0:T(8,128)(2,1)}), bf16[128,32,128]{2,1,0:T(8,128)(2,1)S(1)}, u32[]{:S(2)}, u32[]{:S(2)}) async-start(bf16[128,32,128]{2,1,0:T(8,128)(2,1)} %bitcast.399), calls=%async_computation.9 | async-start | bytes 2097152 | tf_op jit(solution)/shard_map/all_to_all | solution.py:48
  146.7 3.6 convolution_convert_fusion.8
  156.7 3.1 convolution_convert_fusion.5
  165.4 4.3 all-to-all-start.6
  181.0 3.6 all-to-all-done.6
  189.9 4.7 all-to-all-start.7
  194.6 4.6 fusion.73
  207.0 4.0 fusion.26
  213.2 3.1 reshape.607
  216.3 3.7 copy.277
  231.6 3.1 fusion.14
  245.4 4.9 all-to-all-start.10
  250.3 4.1 fusion.19
  262.8 3.6 convolution_convert_fusion.1
  271.7 4.8 all-to-all-start.11
  276.5 3.7 convolution_convert_fusion.2
  284.6 3.1 reshape.618
  289.5 3.5 copy.290
  298.0 3.9 fusion.20
  307.4 4.6 fusion.3
  320.9 3.9 copy.300
  324.8 3.1 copy.301
  328.0 4.9 all-to-all-start.13
  334.8 5.0 pad_maximum_fusion
  339.9 9.5 %all-to-all-start.8 = ((bf16[128,32,128]{2,1,0:T(8,128)(2,1)}), bf16[128,32,128]{2,1,0:T(8,128)(2,1)S(1)}, u32[]{:S(2)}, u32[]{:S(2)}) async-start(bf16[128,32,128]{2,1,0:T(8,128)(2,1)} %bitcast.400), calls=%async_computation.8 | async-start | bytes 2097152 | tf_op jit(solution)/shard_map/all_to_all | solution.py:48
  352.2 8.3 %copy.309 = bf16[1024,2,1408]{2,0,1:T(8,128)(2,1)} copy(bf16[1024,2,1408]{0,2,1:T(8,128)(2,1)} %pad_maximum_fusion) | data formatting | bytes 11534336 | tf_op jit(solution)/shard_map/concatenate | solution.py:229
  360.6 5.7 %copy.310 = bf16[2,8,2,64,1408]{4,3,1,2,0:T(8,128)(2,1)} copy(bf16[2,8,2,64,1408]{4,3,0,1,2:T(8,128)(2,1)} %bitcast.384) | data formatting | bytes 11534336 | tf_op jit(solution)/shard_map/convert_element_type | solution.py:71
  371.6 14.6 %all_to_all.87 = bf16[2,8,2,64,1408]{4,3,1,2,0:T(8,128)(2,1)} all-to-all(bf16[2,8,2,64,1408]{4,3,1,2,0:T(8,128)(2,1)} %copy.310), channel_id=1, replica_groups={{0,8},{16,24},{32,40},{48,56},{64,72},{80,88},{96,104},{112,120},{1,9},..., dimensions={0} | all-to-all | bytes 11534336 | tf_op jit(solution)/shard_map/all_to_all | solution.py:48
  386.2 7.2 %all-to-all-start.14 = ((bf16[16,64,512]{2,1,0:T(8,128)(2,1)}), bf16[16,64,512]{2,1,0:T(8,128)(2,1)S(1)}, u32[]{:S(2)}, u32[]{:S(2)}) async-start(bf16[16,64,512]{2,1,0:T(8,128)(2,1)} %bitcast.114), calls=%async_computation.14 | async-start | bytes 2097152 | tf_op jit(solution)/shard_map/all_to_all | solution.py:48
  393.4 3.9 multiply_reduce_fusion.1
  399.7 11.5 %all-to-all-done.14 = bf16[16,64,512]{2,1,0:T(8,128)(2,1)S(1)} async-done(((bf16[16,64,512]{2,1,0:T(8,128)(2,1)}), bf16[16,64,512]{2,1,0:T(8,128)(2,1)S(1)}, u32[]{:S(2)}, u32[]{:S(2)}) %all-to-all-start.14) | async-done | bytes 1048608 | tf_op jit(solution)/shard_map/all_to_all | solution.py:48
  411.1 6.2 %all-to-all-start.12 = ((bf16[128,32,128]{2,1,0:T(8,128)(2,1)}), bf16[128,32,128]{2,1,0:T(8,128)(2,1)S(1)}, u32[]{:S(2)}, u32[]{:S(2)}) async-start(bf16[128,32,128]{2,1,0:T(8,128)(2,1)} %bitcast.97), calls=%async_computation.12 | async-start | bytes 2097152 | tf_op jit(solution)/shard_map/all_to_all | solution.py:48
  417.3 3.1 fusion.72
  422.9 13.6 %all-to-all-done.12 = bf16[128,32,128]{2,1,0:T(8,128)(2,1)S(1)} async-done(((bf16[128,32,128]{2,1,0:T(8,128)(2,1)}), bf16[128,32,128]{2,1,0:T(8,128)(2,1)S(1)}, u32[]{:S(2)}, u32[]{:S(2)}) %all-to-all-start.12) | async-done | bytes 1048608 | tf_op jit(solution)/shard_map/all_to_all | solution.py:48
  437.5 3.7 all-to-all-start.16
  444.4 66.8 %all-reduce = (f32[1024]{0:T(1024)S(1)}, f32[128]{0:T(128)}, f32[128]{0:T(128)}, f32[1024]{0:T(1024)S(1)}) all-reduce(f32[1024]{0:T(1024)S(1)} %get-tuple-element.15, f32[128]{0:T(128)} %get-tuple-element.17, f32[128]{0:T(128)} %get-tuple-element.19, f32[1024]{0:T(1024)S(1)} %get-tuple-element.13), channel_id=1, replica_groups=mesh['row'=16,'col'=8] {'row'}, use_global_device_ids=true, to_apply=%region_19.20 | all-reduce | flops 2304 | bytes 18432 | tf_op jit(solution)/shard_map/psum | solution.py:283
  511.1 22.7 %all-reduce.1 = (f32[1024]{0:T(1024)}, f32[128]{0:T(128)}, f32[128]{0:T(128)}, f32[1024]{0:T(1024)}) all-reduce(f32[1024]{0:T(1024)S(1)} %get-tuple-element.21, f32[128]{0:T(128)} %get-tuple-element.22, f32[128]{0:T(128)} %get-tuple-element.23, f32[1024]{0:T(1024)S(1)} %get-tuple-element.24), channel_id=1, replica_groups=mesh['row'=16,'col'=8] {'col'}, use_global_device_ids=true, to_apply=%region_20.21 | all-reduce | flops 2304 | bytes 18432 | tf_op jit(solution)/shard_map/psum | solution.py:282
  (297 shorter events, 160.1 us)
Async XLA Ops:
  0.6 26.8 %copy-start = (s32[2,512]{1,0:T(2,128)S(1)}, s32[2,512]{1,0:T(2,128)}, u32[]{:S(2)}) copy-start(s32[2,512]{1,0:T(2,128)} %param.20) | copy-start | bytes 12292
  0.7 14.1 %copy-start.58 = (bf16[2,512,128]{2,1,0:T(8,128)(2,1)S(1)}, bf16[2,512,128]{2,1,0:T(8,128)(2,1)}, u32[]{:S(2)}) copy-start(bf16[2,512,128]{2,1,0:T(8,128)(2,1)} %param.17) | copy-start | bytes 786436
  3.5 15.7 %all-to-all-start.3 = ((s32[16,2,32]{2,1,0:T(2,128)}), s32[16,2,32]{2,1,0:T(2,128)S(1)}, u32[]{:S(2)}, u32[]{:S(2)}) async-start(s32[16,2,32]{2,1,0:T(2,128)} %copy.266), calls=%async_computation.3 | async-start | bytes 32768 | tf_op jit(solution)/shard_map/all_to_all | solution.py:48
  12.0 3.4 copy-start.45
  15.4 8.6 %copy-start.59 = (s32[2,1,4]{2,1,0:T(1,128)S(1)}, s32[2,1,4]{2,1,0:T(1,128)}, u32[]{:S(2)}) copy-start(s32[2,1,4]{2,1,0:T(1,128)} %param.19) | copy-start | bytes 100
  15.5 8.6 %copy-start.60 = (bf16[128]{0:T(256)(128)(2,1)S(1)}, bf16[128]{0:T(256)(128)(2,1)}, u32[]{:S(2)}) copy-start(bf16[128]{0:T(256)(128)(2,1)} %param.26) | copy-start | bytes 772
  15.5 8.6 %copy-start.61 = (bf16[128]{0:T(256)(128)(2,1)S(1)}, bf16[128]{0:T(256)(128)(2,1)}, u32[]{:S(2)}) copy-start(bf16[128]{0:T(256)(128)(2,1)} %param.25) | copy-start | bytes 772
  15.6 11.9 %copy-start.56 = (bf16[1024]{0:T(1024)(128)(2,1)S(1)}, bf16[1024]{0:T(1024)(128)(2,1)}, u32[]{:S(2)}) copy-start(bf16[1024]{0:T(1024)(128)(2,1)} %param.21) | copy-start | bytes 6148
  15.6 11.9 %copy-start.49 = (bf16[384,64]{0,1:T(8,128)(2,1)S(1)}, bf16[384,64]{0,1:T(8,128)(2,1)}, u32[]{:S(2)}) copy-start(bf16[384,64]{0,1:T(8,128)(2,1)} %param.31) | copy-start | bytes 147460
  15.6 11.9 %copy-start.50 = (bf16[64,384]{1,0:T(8,128)(2,1)S(1)}, bf16[64,384]{1,0:T(8,128)(2,1)}, u32[]{:S(2)}) copy-start(bf16[64,384]{1,0:T(8,128)(2,1)} %param.30) | copy-start | bytes 147460
  15.6 11.9 %copy-start.51 = (bf16[64,384]{1,0:T(8,128)(2,1)S(1)}, bf16[64,384]{1,0:T(8,128)(2,1)}, u32[]{:S(2)}) copy-start(bf16[64,384]{1,0:T(8,128)(2,1)} %param.29) | copy-start | bytes 147460
  15.6 11.9 %copy-start.53 = (bf16[256,64]{0,1:T(8,128)(2,1)S(1)}, bf16[256,64]{0,1:T(8,128)(2,1)}, u32[]{:S(2)}) copy-start(bf16[256,64]{0,1:T(8,128)(2,1)} %param.27) | copy-start | bytes 98308
  20.4 21.9 %all-to-all-start.1 = ((bf16[16,64,512]{2,1,0:T(8,128)(2,1)}), bf16[16,64,512]{2,1,0:T(8,128)(2,1)S(1)}, u32[]{:S(2)}, u32[]{:S(2)}) async-start(bf16[16,64,512]{2,1,0:T(8,128)(2,1)} %broadcast_in_dim.59), calls=%async_computation.1 | async-start | bytes 2097152 | tf_op jit(solution)/shard_map/all_to_all | solution.py:48
  49.1 25.3 %all-to-all-start = ((bf16[128,32,128]{2,1,0:T(8,128)(2,1)}), bf16[128,32,128]{2,1,0:T(8,128)(2,1)S(1)}, u32[]{:S(2)}, u32[]{:S(2)}) async-start(bf16[128,32,128]{2,1,0:T(8,128)(2,1)} %bitcast.398), calls=%async_computation | async-start | bytes 2097152 | tf_op jit(solution)/shard_map/all_to_all | solution.py:48
  61.3 13.1 %copy-start.44 = (bf16[64,1408]{1,0:T(8,128)(2,1)S(1)}, bf16[64,1408]{1,0:T(8,128)(2,1)}, u32[]{:S(2)}) copy-start(bf16[64,1408]{1,0:T(8,128)(2,1)} %pad_maximum_fusion.5) | copy-start | bytes 540676
  76.3 48.7 %all-to-all-start.4 = ((bf16[16,64,1408]{2,1,0:T(8,128)(2,1)}), bf16[16,64,1408]{2,1,0:T(8,128)(2,1)}, u32[]{:S(2)}, u32[]{:S(2)}) async-start(bf16[16,64,1408]{2,1,0:T(8,128)(2,1)} %broadcast_in_dim.72), calls=%async_computation.4 | async-start | bytes 5767168 | tf_op jit(solution)/shard_map/all_to_all | solution.py:48
  82.6 2.8 copy-start.4
  88.0 4.3 copy-start.29
  127.6 9.6 %copy-start.37 = (bf16[16,2,32,128]{3,2,1,0:T(8,128)(2,1)S(1)}, bf16[16,2,32,128]{3,2,1,0:T(8,128)(2,1)}, u32[]{:S(2)}) copy-start(bf16[16,2,32,128]{3,2,1,0:T(8,128)(2,1)} %copy.282) | copy-start | bytes 786436
  138.4 27.0 %all-to-all-start.9 = ((bf16[128,32,128]{2,1,0:T(8,128)(2,1)}), bf16[128,32,128]{2,1,0:T(8,128)(2,1)S(1)}, u32[]{:S(2)}, u32[]{:S(2)}) async-start(bf16[128,32,128]{2,1,0:T(8,128)(2,1)} %bitcast.399), calls=%async_computation.9 | async-start | bytes 2097152 | tf_op jit(solution)/shard_map/all_to_all | solution.py:48
  144.7 5.6 %slice-start = ((s8[5767168]{0:T(1024)(128)(4,1)}), s8[4194304]{0:T(1024)(128)(4,1)S(1)}, s32[]{:S(2)}) async-start(s8[5767168]{0:T(1024)(128)(4,1)} %bitcast.381), calls=%async_computation.17 | async-start | bytes 8388608
  146.7 3.6 copy-start.62
  146.7 3.6 slice-start.1
  162.4 7.3 %copy-start.57 = (bf16[1024]{0:T(1024)(128)(2,1)S(1)}, bf16[1024]{0:T(1024)(128)(2,1)}, u32[]{:S(2)}) copy-start(bf16[1024]{0:T(1024)(128)(2,1)} %param.28) | copy-start | bytes 6148
  165.4 19.3 %all-to-all-start.6 = ((bf16[4,512,2,128]{3,2,1,0:T(2,128)(2,1)}), bf16[4,512,2,128]{3,2,1,0:T(2,128)(2,1)}, u32[]{:S(2)}, u32[]{:S(2)}) async-start(bf16[4,512,2,128]{3,2,1,0:T(2,128)(2,1)} %bitcast.403), calls=%async_computation.6 | async-start | bytes 2097152 | tf_op jit(solution)/shard_map/all_to_all | solution.py:48
  189.9 26.4 %all-to-all-start.7 = ((bf16[4,512,2,128]{3,2,1,0:T(2,128)(2,1)}), bf16[4,512,2,128]{3,2,1,0:T(2,128)(2,1)}, u32[]{:S(2)}, u32[]{:S(2)}) async-start(bf16[4,512,2,128]{3,2,1,0:T(2,128)(2,1)} %broadcast_in_dim.74), calls=%async_computation.7 | async-start | bytes 2097152 | tf_op jit(solution)/shard_map/all_to_all | solution.py:48
  207.0 4.0 copy-start.11
  207.0 4.0 copy-start.25
  230.0 4.8 copy-start.65
  245.4 21.1 %all-to-all-start.10 = ((bf16[4,512,2,128]{3,2,1,0:T(2,128)(2,1)}), bf16[4,512,2,128]{3,2,1,0:T(2,128)(2,1)}, u32[]{:S(2)}, u32[]{:S(2)}) async-start(bf16[4,512,2,128]{3,2,1,0:T(2,128)(2,1)} %bitcast.404), calls=%async_computation.10 | async-start | bytes 2097152 | tf_op jit(solution)/shard_map/all_to_all | solution.py:48
  271.7 17.9 %all-to-all-start.11 = ((bf16[4,512,2,128]{3,2,1,0:T(2,128)(2,1)}), bf16[4,512,2,128]{3,2,1,0:T(2,128)(2,1)}, u32[]{:S(2)}, u32[]{:S(2)}) async-start(bf16[4,512,2,128]{3,2,1,0:T(2,128)(2,1)} %broadcast_in_dim.78), calls=%async_computation.11 | async-start | bytes 2097152 | tf_op jit(solution)/shard_map/all_to_all | solution.py:48
  276.5 3.8 copy-start.38
  276.5 3.8 copy-start.43
  298.0 3.9 copy-start.14
  298.0 3.9 copy-start.63
  307.4 4.6 copy-start.42
  328.0 5.0 copy-start.39
  328.0 11.9 %all-to-all-start.13 = ((bf16[2,8,2,64,512]{4,3,1,2,0:T(8,128)(2,1)}), bf16[2,8,2,64,512]{4,3,1,2,0:T(8,128)(2,1)}, u32[]{:S(2)}, u32[]{:S(2)}) async-start(bf16[2,8,2,64,512]{4,3,1,2,0:T(8,128)(2,1)} %copy.301), calls=%async_computation.13 | async-start | bytes 4194304 | tf_op jit(solution)/shard_map/all_to_all | solution.py:48
  339.9 31.7 %all-to-all-start.8 = ((bf16[128,32,128]{2,1,0:T(8,128)(2,1)}), bf16[128,32,128]{2,1,0:T(8,128)(2,1)S(1)}, u32[]{:S(2)}, u32[]{:S(2)}) async-start(bf16[128,32,128]{2,1,0:T(8,128)(2,1)} %bitcast.400), calls=%async_computation.8 | async-start | bytes 2097152 | tf_op jit(solution)/shard_map/all_to_all | solution.py:48
  371.6 14.6 %copy-start.17 = (bf16[128,32,128]{2,1,0:T(8,128)(2,1)}, bf16[128,32,128]{2,1,0:T(8,128)(2,1)S(1)}, u32[]{:S(2)}) copy-start(bf16[128,32,128]{2,1,0:T(8,128)(2,1)S(1)} %all-to-all-done.8) | copy-start | bytes 3145732
  386.2 7.2 %copy-start.35 = (bf16[2,128,512]{2,1,0:T(8,128)(2,1)S(1)}, bf16[2,128,512]{2,1,0:T(8,128)(2,1)}, u32[]{:S(2)}) copy-start(bf16[2,128,512]{2,1,0:T(8,128)(2,1)} %fusion.20) | copy-start | bytes 786436
  386.2 25.0 %all-to-all-start.14 = ((bf16[16,64,512]{2,1,0:T(8,128)(2,1)}), bf16[16,64,512]{2,1,0:T(8,128)(2,1)S(1)}, u32[]{:S(2)}, u32[]{:S(2)}) async-start(bf16[16,64,512]{2,1,0:T(8,128)(2,1)} %bitcast.114), calls=%async_computation.14 | async-start | bytes 2097152 | tf_op jit(solution)/shard_map/all_to_all | solution.py:48
  393.4 3.9 copy-start.7
  411.1 9.3 %copy-start.20 = (bf16[16,64,512]{2,1,0:T(8,128)(2,1)}, bf16[16,64,512]{2,1,0:T(8,128)(2,1)S(1)}, u32[]{:S(2)}) copy-start(bf16[16,64,512]{2,1,0:T(8,128)(2,1)S(1)} %all-to-all-done.14) | copy-start | bytes 3145732
  411.1 25.3 %all-to-all-start.12 = ((bf16[128,32,128]{2,1,0:T(8,128)(2,1)}), bf16[128,32,128]{2,1,0:T(8,128)(2,1)S(1)}, u32[]{:S(2)}, u32[]{:S(2)}) async-start(bf16[128,32,128]{2,1,0:T(8,128)(2,1)} %bitcast.97), calls=%async_computation.12 | async-start | bytes 2097152 | tf_op jit(solution)/shard_map/all_to_all | solution.py:48
  436.5 6.2 %copy-start.46 = (pred[2,512,512]{2,1,0:T(32,128)(4,1)S(1)}, pred[2,512,512]{2,1,0:T(32,128)(4,1)}, u32[]{:S(2)}) copy-start(pred[2,512,512]{2,1,0:T(32,128)(4,1)} %copy-done.45) | copy-start | bytes 1572868
  437.5 101.2 %all-to-all-start.16 = ((bf16[16,64,1408]{2,1,0:T(8,128)(2,1)}), bf16[16,64,1408]{2,1,0:T(8,128)(2,1)S(1)}, u32[]{:S(2)}, u32[]{:S(2)}) async-start(bf16[16,64,1408]{2,1,0:T(8,128)(2,1)} %bitcast.128), calls=%async_computation.16 | async-start | bytes 5767168 | tf_op jit(solution)/shard_map/all_to_all | solution.py:48
  533.8 2.8 copy-start.19
  (35 other events, 55.0 us)
